TPU v7x, 128 devices: a whole 4x4x4 slice. The times are simulated.
128 devices in a mesh: py: 8 (over x_hi, z), pz: 16 (over x_lo, y, core).
Axes of the slice: x: 4 (x_hi: 2, x_lo: 2; x = x_hi * 2 + x_lo), y: 4, z: 4, core: 2. Of those that a mesh axis runs over, the one named last changes fastest.
Arguments:
- conserved: float32 [5, 512, 256, 256], P(None, 'pz', 'py'), may hold values from -2 to 3.5, as said below
- register: float32 [5, 512, 256, 256], P(None, 'pz', 'py'), may hold values from -6 to 6
- stream_blocks: float32 [2, 3, 128, 128], replicated, may hold values from -0.3125 to 0.3125
- wall_matrix: float32 [256, 256], replicated, may hold values from -0.375 to 0.375
- span_blocks: float32 [16, 3, 32, 32], replicated, may hold values from -0.625 to 0.625
- inflow_gain: float32 [5], replicated, may hold values from 0.5 to 2
- source_block: int32 [128, 1024, 1], replicated, may hold values from 0 to 127; in each aligned block of 1024 rows (0 to 1023, 1024 to 2047, ..., all dimensions but the last counted through in order) at most 16 rows name the same one
- source_column: int32 [128, 1024], replicated, may hold values from 0 to 1023
Outputs:
- new_conserved: float32 [5, 512, 256, 256], P(None, 'pz', 'py')
- new_register: float32 [5, 512, 256, 256], P(None, 'pz', 'py')
Inputs may be any that keep to these rules, and one draw needn't show every extreme that they name: Among the 1024 entries of one column block, source_block[b, :, 0], no value appears more than 16 times, and in some column block one value appears exactly 16 times. `conserved`: the first field, the density, lies between 0.5 and 2.
All inputs are finite; a program needn't handle non-finite values.
Results may differ from a plain program's by a relative error of at most 0.0001.
Values sent between devices are 32-bit elements; how exact they have to be, the bound alone decides.
A program may use at most 192 MiB of HBM per device.

v0:
```python
import jax
import jax.numpy as jnp
from jax import lax
from jax.sharding import PartitionSpec as P

highest = lax.Precision.HIGHEST
section_decay = -5.0 / 9.0
section_gain = 15.0 / 16.0
time_step = 0.1


def flux_set(values, direction):
    speeds = values[1:4] / values[0]
    pressure = 0.4 * (
        values[4] - 0.5 * (values[1] * speeds[0] + values[2] * speeds[1] + values[3] * speeds[2])
    )
    velocity = speeds[direction]
    pieces = [values[1 + direction]]
    for component in range(1, 4):
        moment = values[component] * velocity
        if component - 1 == direction:
            moment = moment + pressure
        pieces.append(moment)
    pieces.append((values[4] + pressure) * velocity)
    return jnp.stack(pieces)


def stream_derivative(values, blocks):
    leading = values.shape[:-1]
    block_count = blocks.shape[0]
    block_width = blocks.shape[2]
    shaped = values.reshape(leading + (block_count, block_width))
    summed = jnp.einsum("kab,...kb->...ka", blocks[:, 1], shaped, precision=highest)
    lower = jnp.einsum("kab,...kb->...ka", blocks[1:, 0], shaped[..., :-1, :], precision=highest)
    upper = jnp.einsum("kab,...kb->...ka", blocks[:-1, 2], shaped[..., 1:, :], precision=highest)
    zero_block = jnp.zeros(leading + (1, block_width), jnp.float32)
    summed = (
        summed
        + jnp.concatenate([zero_block, lower], axis=-2)
        + jnp.concatenate([upper, zero_block], axis=-2)
    )
    return summed.reshape(values.shape)


def wall_derivative(values, matrix):
    return jnp.einsum("ab,fzbx->fzax", matrix, values, precision=highest)


def span_derivative(values, blocks):
    block_count = blocks.shape[0]
    block_width = blocks.shape[2]
    shaped = values.reshape((values.shape[0], block_count, block_width) + values.shape[2:])
    summed = jnp.zeros(shaped.shape, jnp.float32)
    for offset in range(3):
        rolled = jnp.roll(shaped, 1 - offset, axis=1)
        summed = summed + jnp.einsum(
            "kab,fkb...->fka...", blocks[:, offset], rolled, precision=highest
        )
    return summed.reshape(values.shape)


def local(
    conserved,
    register,
    stream_blocks,
    wall_matrix,
    span_blocks,
    inflow_gain,
    source_block,
    source_column,
):
    field_count, span_local, wall_local, stream_cells = conserved.shape
    column_count = span_local * wall_local
    recycle_index = 3 * stream_cells // 4
    recycle = conserved[:, :, :, recycle_index].reshape(field_count, column_count)
    myself = lax.axis_index(("py", "pz"))
    own_anchor = lax.dynamic_index_in_dim(source_block[:, :, 0], myself, 0, keepdims=False)
    own_column = lax.dynamic_index_in_dim(source_column, myself, 0, keepdims=False)
    whole_plane = lax.all_gather(recycle, ("py", "pz"), axis=1, tiled=True)
    fetched = jnp.take(whole_plane, own_anchor * column_count + own_column, axis=1)
    inlet_plane = (fetched * inflow_gain[:, None]).reshape(field_count, span_local, wall_local)
    current = conserved.at[:, :, :, 0].set(inlet_plane)
    stream_term = stream_derivative(flux_set(current, 0), stream_blocks)
    by_rows = lax.all_to_all(current, "py", split_axis=1, concat_axis=2, tiled=True)
    wall_term = wall_derivative(flux_set(by_rows, 1), wall_matrix)
    returned = lax.all_to_all(wall_term, "py", split_axis=2, concat_axis=1, tiled=True)
    span_term = span_derivative(
        flux_set(lax.all_to_all(current, "pz", split_axis=2, concat_axis=1, tiled=True), 2),
        span_blocks,
    )
    side_term = lax.all_to_all(span_term, "pz", split_axis=1, concat_axis=2, tiled=True)
    combined = stream_term + returned + side_term
    new_register = section_decay * register - time_step * combined
    new_conserved = current + section_gain * new_register
    return (new_conserved, new_register)


def solution(mesh):
    return jax.shard_map(
        local,
        mesh=mesh,
        in_specs=(
            P(None, "pz", "py", None),
            P(None, "pz", "py", None),
            P(),
            P(),
            P(),
            P(),
            P(),
            P(),
        ),
        out_specs=(P(None, "pz", "py", None), P(None, "pz", "py", None)),
        check_vma=False,
    )
```

profile of v0, /device:TPU:0, one launch (start us, length us, event | category | flops | bytes accessed | tf_op | source)
XLA Modules:
  0.0 758.4 jit_solution(9412366285971812997)
XLA Ops:
  7.2 2.5 copy.191
  9.8 2.4 copy-done.2
  12.8 6.9 copy.100
  22.2 368.2 %all-gather.2.cloned.1.call-done = f32[5,131072]{0,1:T(8,128)} async-done(((f32[5,1024]{0,1:T(8,128)}), f32[5,131072]{0,1:T(8,128)}) %all-gather.2.cloned.1.call-update) | async-done | bytes 2621456 | tf_op jit(solution)/shard_map/all_gather | solution.py:79
  390.4 10.5 %gather_fusion = f32[1024,5]{1,0:T(8,128)S(1)} fusion(f32[5,131072]{0,1:T(8,128)} %all-gather.2.cloned.1.call-done, s32[1024]{0:T(1024)S(1)} %broadcast_clamp_fusion), kind=kCustom, calls=%fused_computation | custom fusion | bytes 45056 | tf_op jit(solution)/shard_map/jit(_take)/gather | solution.py:80
  400.9 8.9 %copy.101 = f32[5,32,32,1]{3,2,1,0:T(8,128)} copy(f32[5,32,32,1]{0,2,1,3:T(8,128)S(1)} %bitcast.187) | data formatting | bytes 40960 | tf_op jit(solution)/shard_map/jit(_take)/gather | solution.py:80
  409.8 2.3 select_multiply_fusion
  412.1 7.4 scatter.4
  419.5 5.7 copy.109
  425.1 6.7 all-to-all-start
  431.8 7.9 %copy.130 = f32[5,32,32,256]{3,1,0,2:T(8,128)} copy(f32[5,32,32,256]{3,2,1,0:T(8,128)} %scatter.4) | data formatting | bytes 10485760 | tf_op jit(solution)/shard_map/scatter | solution.py:82
  439.7 52.1 %all-to-all-done = f32[5,32,32,256]{3,2,0,1:T(8,128)} async-done(((f32[5,32,32,256]{3,2,0,1:T(8,128)}), f32[5,32,32,256]{3,2,0,1:T(8,128)}, u32[]{:S(2)}, u32[]{:S(2)}) %all-to-all-start) | async-done | bytes 5242912 | tf_op jit(solution)/shard_map/all_to_all | solution.py:84
  491.8 4.6 all-to-all-start.2
  496.4 2.9 copy.110
  502.7 2.6 copy.126
  505.3 2.3 copy.112
  507.6 2.5 copy.117
  512.1 2.4 copy.116
  514.5 2.3 copy.114
  516.8 2.5 copy.115
  519.3 2.4 copy.119
  521.8 2.5 copy.123
  524.3 2.4 copy.121
  526.6 2.6 copy.122
  533.7 6.1 convolution_bitcast_fusion
  539.8 7.3 copy.127
  547.0 21.7 %all-to-all-done.2 = f32[5,32,32,256]{3,1,0,2:T(8,128)} async-done(((f32[5,32,32,256]{3,1,0,2:T(8,128)}), f32[5,32,32,256]{3,1,0,2:T(8,128)}, u32[]{:S(2)}, u32[]{:S(2)}) %all-to-all-start.2) | async-done | bytes 5242912 | tf_op jit(solution)/shard_map/all_to_all | solution.py:88
  568.7 6.7 all-to-all-start.1
  575.4 3.1 copy.176
  582.2 3.3 fusion.59
  585.5 5.1 fusion.3
  590.6 5.3 fusion.38
  595.8 7.6 %add_bitcast_fusion = f32[5,16,32,2,256]{4,2,3,0,1:T(8,128)S(1)} fusion(f32[16,5,2,256,32]{3,4,2,1,0:T(8,128)S(1)} %fusion.3, f32[16,5,2,256,32]{3,4,2,1,0:T(8,128)S(1)} %fusion.38, f32[5,1,32,2,256]{4,2,3,0,1:T(8,128)S(1)} %get-tuple-element.33, f32[5,15,32,2,256]{4,2,3,0,1:T(8,128)} %get-tuple-element.31, f32[16,3,32,32]{3,2,1,0:T(8,128)S(1)} %copy-done.10), kind=kOutput, calls=%fused_computation.18 | convolution fusion | flops 507248640 | bytes 21233664 | tf_op jit(solution)/shard_map/kab,fkb...->fka.../dot_general | solution.py:56
  603.9 6.4 copy.147
  610.3 24.7 %all-to-all-done.1 = f32[5,4,256,256]{3,1,0,2:T(4,128)} async-done(((f32[5,4,256,256]{3,1,0,2:T(4,128)}), f32[5,4,256,256]{3,1,0,2:T(4,128)}, u32[]{:S(2)}, u32[]{:S(2)}) %all-to-all-start.1) | async-done | bytes 5242912 | tf_op jit(solution)/shard_map/all_to_all | solution.py:86
  635.0 10.9 %all-to-all-start.3 = ((f32[5,512,2,256]{3,2,0,1:T(2,128)}), f32[5,512,2,256]{3,2,0,1:T(2,128)}, u32[]{:S(2)}, u32[]{:S(2)}) async-start(f32[5,512,2,256]{3,2,0,1:T(2,128)} %copy.147), calls=%async_computation.3 | async-start | bytes 10485760 | tf_op jit(solution)/shard_map/all_to_all | solution.py:91
  647.3 2.8 slice_divide_fusion
  650.1 3.2 add_multiply_fusion
  655.5 2.7 stack.39
  658.2 2.8 stack.40
  673.3 6.3 fusion.12
  679.6 3.4 copy.128
  683.0 2.8 copy.129
  685.8 33.5 %all-to-all-done.3 = f32[5,512,2,256]{3,2,0,1:T(2,128)} async-done(((f32[5,512,2,256]{3,2,0,1:T(2,128)}), f32[5,512,2,256]{3,2,0,1:T(2,128)}, u32[]{:S(2)}, u32[]{:S(2)}) %all-to-all-start.3) | async-done | bytes 5242912 | tf_op jit(solution)/shard_map/all_to_all | solution.py:91
  719.3 3.0 copy.148
  722.3 6.4 copy.149
  728.7 7.6 %all_to_all.61 = f32[5,32,32,256]{3,2,1,0:T(8,128)} reshape(f32[5,32,16,2,256]{4,3,2,1,0:T(2,128)} %copy.149) | data formatting | bytes 10485760 | tf_op jit(solution)/shard_map/all_to_all | solution.py:91
  736.4 14.8 %multiply_add_fusion = (f32[5,32,32,256]{3,2,1,0:T(8,128)}, f32[5,32,32,256]{3,2,1,0:T(8,128)}) fusion(f32[5,32,32,256]{3,2,1,0:T(8,128)} %scatter.4, f32[5,32,32,256]{3,2,1,0:T(8,128)} %all_to_all.61, f32[5,32,32,256]{3,2,1,0:T(8,128)} %bitcast.171, f32[2,5,32,4,8,128]{5,4,3,2,1,0:T(8,128)} %fusion.12, f32[5,32,32,256]{3,2,1,0:T(8,128)} %param.11), kind=kLoop, calls=%fused_computation.17 | loop fusion | flops 9175040 | bytes 36700160 | tf_op jit(solution)/shard_map/add | solution.py:94
  (79 shorter events, 32.6 us)
Async XLA Ops:
  7.2 526.6 %copy-start = (f32[256,256]{1,0:T(8,128)S(1)}, f32[256,256]{1,0:T(8,128)}, u32[]{:S(2)}) copy-start(f32[256,256]{1,0:T(8,128)} %param.13) | copy-start | bytes 786436
  7.2 383.2 %all-gather.2.cloned.1.call-start = ((), (), s32[]{:S(2)}) async-start(), calls=%async_computation.4 | async-start | bytes 67633152 | tf_op jit(solution)/shard_map/all_gather | solution.py:79
  9.7 2.4 copy-start.2
  12.1 397.7 %copy-start.12 = (f32[5]{0:T(128)S(1)}, f32[5]{0:T(128)}, u32[]{:S(2)}) copy-start(f32[5]{0:T(128)} %param.15) | copy-start | bytes 64
  425.1 66.7 %all-to-all-start = ((f32[5,32,32,256]{3,2,0,1:T(8,128)}), f32[5,32,32,256]{3,2,0,1:T(8,128)}, u32[]{:S(2)}, u32[]{:S(2)}) async-start(f32[5,32,32,256]{3,2,0,1:T(8,128)} %copy.109), calls=%async_computation | async-start | bytes 10485760 | tf_op jit(solution)/shard_map/all_to_all | solution.py:84
  491.8 76.9 %all-to-all-start.2 = ((f32[5,32,32,256]{3,1,0,2:T(8,128)}), f32[5,32,32,256]{3,1,0,2:T(8,128)}, u32[]{:S(2)}, u32[]{:S(2)}) async-start(f32[5,32,32,256]{3,1,0,2:T(8,128)} %copy.130), calls=%async_computation.2 | async-start | bytes 10485760 | tf_op jit(solution)/shard_map/all_to_all | solution.py:88
  529.3 3.2 copy-start.3
  530.7 2.0 copy-start.4
  530.7 2.0 copy-start.5
  530.7 2.2 copy-start.6
  568.7 66.3 %all-to-all-start.1 = ((f32[5,4,256,256]{3,1,0,2:T(4,128)}), f32[5,4,256,256]{3,1,0,2:T(4,128)}, u32[]{:S(2)}, u32[]{:S(2)}) async-start(f32[5,4,256,256]{3,1,0,2:T(4,128)} %copy.127), calls=%async_computation.1 | async-start | bytes 10485760 | tf_op jit(solution)/shard_map/all_to_all | solution.py:86
  582.2 3.3 copy-start.10
  635.0 84.3 %all-to-all-start.3 = ((f32[5,512,2,256]{3,2,0,1:T(2,128)}), f32[5,512,2,256]{3,2,0,1:T(2,128)}, u32[]{:S(2)}, u32[]{:S(2)}) async-start(f32[5,512,2,256]{3,2,0,1:T(2,128)} %copy.147), calls=%async_computation.3 | async-start | bytes 10485760 | tf_op jit(solution)/shard_map/all_to_all | solution.py:91
  647.2 6.0 slice-start
  650.0 3.2 slice-start.1
  662.5 5.9 copy-start.7
  664.0 4.5 copy-start.8
  665.6 3.1 copy-start.9
  665.6 3.3 copy-start.11
  736.4 14.8 %copy-start.1 = (f32[256,256]{1,0:T(8,128)S(1)}, f32[256,256]{1,0:T(8,128)}, u32[]{:S(2)}) copy-start(f32[256,256]{1,0:T(8,128)} %param.13) | copy-start | bytes 786436
Sparse Core Ops, SparseCore 0:
  19.8 370.4 all-gather.1
where the time goes:
time: 773 us; the launch traced here: 758 us
  waiting for transfers between devices  500 us (65%)
  local copies, waits for them, and re-layouts  149 us (19%)
  matrix products  34.7 us (4%)
  other arithmetic  30.7 us (4%)
  starting transfers between devices  28.9 us (4%)
  between operations  15 us (2%)
    all_gather x1, waiting for transfers between devices, local(): whole_plane = lax.all_gather(recycle, ('py', 'pz'), axis=1, tiled=True)  368 us
    all_to_all x1, waiting for transfers between devices, local(): lax.all_to_all(current, 'py', split_axis=1, concat_axis=2, tiled=True)  52.1 us
    all_to_all x1, waiting for transfers between devices, local(): lax.all_to_all(span_term, 'pz', split_axis=1, concat_axis=2, tiled=True)  33.5 us
    all_to_all x1, waiting for transfers between devices, local(): lax.all_to_all(wall_term, 'py', split_axis=2, concat_axis=1, tiled=True)  24.7 us
    all_to_all x1, waiting for transfers between devices, local(): lax.all_to_all(current, 'pz', split_axis=2, concat_axis=1, tiled=True)  21.7 us
    scatter x3, local copies, waits for them, and re-layouts, local(): current = conserved.at[:, :, :, 0].set(inlet_plane)  20.9 us
    gather x2, local copies, waits for them, and re-layouts, local(): jnp.take(whole_plane, own_anchor * column_count + own_column, axis=1)  19.4 us
    dot_general x3, matrix products, span_derivative(): jnp.einsum('kab,fkb...->fka...', blocks[:, offset], rolled, precision=hig...  17.9 us
  transfers between devices with their start and end apart: 5, of which 5 were waited for; matrix products, arithmetic and copies ran while one was open for 18% of the time, Pallas kernels for 0%

commit v1 on v0

v1 whole, which is shorter than its diff:
```python
import functools

import jax
import jax.numpy as jnp
from jax import lax
from jax.experimental import pallas as pl
from jax.experimental.pallas import tpu as pltpu
from jax.sharding import PartitionSpec as P

MESH = pl.DeviceIdType.MESH
F32 = jnp.float32
BF16 = jnp.bfloat16
SECTION_DECAY = -5.0 / 9.0
SECTION_GAIN = 15.0 / 16.0
TIME_STEP = 0.1
ORDER = (4, 1, 3, 5, 7, 6, 2)


def flux(direction, density, first, second, third, energy):
    inverse = 1.0 / density
    moments = (first, second, third)
    speeds = tuple(moment * inverse for moment in moments)
    pressure = 0.4 * (
        energy - 0.5 * (first * speeds[0] + second * speeds[1] + third * speeds[2])
    )
    velocity = speeds[direction]
    pieces = [moments[direction]]
    for component in range(3):
        moment = moments[component] * velocity
        if component == direction:
            moment = moment + pressure
        pieces.append(moment)
    pieces.append((energy + pressure) * velocity)
    return pieces


def halves(value):
    high = value.astype(BF16)
    return high, (value - high.astype(F32)).astype(BF16)


def thirds(value):
    high = value.astype(BF16)
    rest = value - high.astype(F32)
    middle = rest.astype(BF16)
    return high, middle, (rest - middle.astype(F32)).astype(BF16)


def mm(left, right):
    return jnp.dot(left, right, preferred_element_type=F32)


def iota(shape, axis):
    return lax.broadcasted_iota(jnp.int32, shape, axis)


def kernel(
    con,
    reg,
    stream_in,
    wall_in,
    span_in,
    gain,
    source_block,
    source_column,
    out_con,
    out_reg,
    cur,
    got,
    wall_out,
    back,
    base,
    halo,
    work,
    stream_work,
    wall_w,
    stream_w,
    span_w,
    slot_key,
    picked,
    staged,
    received,
    load_sem,
    fs,
    fr,
    bs,
    br,
    hs,
    hr,
    s1s,
    s1r,
    s2s,
    s2r,
    out_sem,
):
    py, pz = lax.axis_index("py"), lax.axis_index("pz")
    me = py * 16 + pz

    def peer(offset):
        return lax.rem(py // 4 + offset // 4, 2) * 4 + lax.rem(lax.rem(py, 4) + offset % 4, 4)

    def half(h):
        return pl.ds(128 * h, 128)

    def remote(src, dst, send, recv, device):
        return pltpu.make_async_remote_copy(
            src_ref=src,
            dst_ref=dst,
            send_sem=send,
            recv_sem=recv,
            device_id=device,
            device_id_type=MESH,
        )

    def forward(h, q, offset):
        p = peer(offset)
        src = con.at[:, p, q, :, half(1)] if h == 1 else cur.at[0, :, p, q]
        return remote(
            src, got.at[h, q, :, py], fs.at[h, q, offset], fr.at[h, q, offset], (p, pz)
        )

    def own(h, q):
        src = con.at[:, py, q, :, half(1)] if h == 1 else cur.at[0, :, py, q]
        return pltpu.make_async_copy(src, got.at[h, q, :, py], fr.at[h, q, 0])

    def giveback(h, q, offset):
        p = peer(offset)
        return remote(
            wall_out.at[h, q, :, p],
            back.at[h, :, py, q],
            bs.at[h, q, offset],
            br.at[h, q, offset],
            (p, pz),
        )

    def beside(h, side, i):
        rows = pl.ds(2 * i, 2)
        src = con.at[:, rows, :, :, half(1)] if h == 1 else cur.at[0, :, rows]
        target = lax.rem(pz + (1 if side == 0 else 15), 16)
        return remote(
            src, halo.at[side, h, :, rows], hs.at[h, side, i], hr.at[h, side, i], (py, target)
        )

    def send_forward(h, q):
        own(h, q).start()
        for offset in ORDER:
            forward(h, q, offset).start()

    def send_beside(h, i):
        for side in range(2):
            beside(h, side, i).start()

    def stage_one(offset):
        p = peer(offset)
        return remote(
            picked.at[p], staged.at[:, py], s1s.at[offset], s1r.at[offset], (p, pz)
        )

    def stage_two(offset):
        target = lax.rem(pz + offset, 16)
        return remote(
            staged.at[target], received.at[pz], s2s.at[offset], s2r.at[offset], (py, target)
        )

    loads = [
        pltpu.make_async_copy(con.at[:, :, :, :, half(h)], cur.at[h], load_sem.at[h])
        for h in (1, 0)
    ] + [
        pltpu.make_async_copy(reg.at[:, :, :, :, half(h)], base.at[h], load_sem.at[2 + h])
        for h in range(2)
    ]
    for load in loads:
        load.start()

    barrier = pltpu.get_barrier_semaphore()
    for offset in range(1, 8):
        pl.semaphore_signal(barrier, inc=1, device_id=(peer(offset), pz), device_id_type=MESH)
    for offset in range(1, 16):
        pl.semaphore_signal(
            barrier, inc=1, device_id=(py, lax.rem(pz + offset, 16)), device_id_type=MESH
        )
    pl.semaphore_wait(barrier, 22)

    send_forward(1, 0)
    send_beside(1, 0)
    send_forward(1, 1)

    lane = iota((128, 128), 1)
    row = iota((128, 128), 0)
    strict = jnp.where(row < lane, 1.0, 0.0).astype(BF16)
    counts = jnp.concatenate([strict, jnp.ones((128, 128), BF16)], axis=1)
    passed = jnp.zeros((128, 128), F32)
    for g in range(8):
        mine = source_block[:, 128 * g : 128 * g + 128] == me
        ranked = mm(jnp.where(mine, 1.0, 0.0).astype(BF16), counts)
        slot_key[:, 128 * g : 128 * g + 128] = jnp.where(mine, ranked[:, :128] + passed, -1.0)
        passed = passed + ranked[:, 128:]

    loads[0].wait()
    for g in range(8):
        plane = jnp.zeros((128, 128), F32)
        for f in range(5):
            value = cur[1, f, g].reshape(128, 128)
            plane = plane + jnp.where(
                lane == f, jnp.broadcast_to(value[:, 64:65], (128, 128)), 0.0
            )
        for part, piece in enumerate(thirds(plane)):
            work[pl.ds(128 * g, 128), 128 * part : 128 * part + 128] = piece

    def pick(r, carry):
        total = jnp.zeros((128, 128), F32)
        for g in range(8):
            columns = source_column[:, 128 * g : 128 * g + 128].astype(F32)
            total = total + jnp.where(
                slot_key[:, 128 * g : 128 * g + 128] == r.astype(F32), columns, 0.0
            )
        wanted = jnp.sum(total, axis=1, keepdims=True)
        choose = jnp.concatenate(
            [
                jnp.where((lane + 128 * g).astype(F32) == wanted, 1.0, 0.0).astype(BF16)
                for g in range(8)
            ],
            axis=1,
        )
        values = mm(choose, work[pl.ds(0, 1024), 0:384])
        values = values[:, :128] + values[:, 128:256] + values[:, 256:384]
        return carry + pltpu.roll(values, 8 * r, 1)

    picked[...] = lax.fori_loop(0, 16, pick, jnp.zeros((128, 128), F32)).reshape(8, 16, 128)

    for offset in range(1, 8):
        stage_one(offset).start()
    for p in range(8):

        @pl.when(py == p)
        def _(p=p):
            staged[:, p, :] = picked[p]

    send_forward(1, 2)
    send_beside(1, 1)

    high, low = halves(wall_in[...])
    wall_w[:, 0:256] = high
    wall_w[:, 256:512] = high
    wall_w[:, 512:768] = low
    for k in range(2):
        for j in range(2):
            high, low = halves(stream_in[k, j - k + 1])
            rows = slice(128 * k, 128 * k + 128)
            stream_w[rows, 128 * j : 128 * j + 128] = high
            stream_w[rows, 256 + 128 * j : 256 + 128 * j + 128] = high
            stream_w[rows, 512 + 128 * j : 512 + 128 * j + 128] = low
    spread = jnp.where(iota((256, 32), 0) // 8 == iota((256, 32), 1), 1.0, 0.0).astype(BF16)
    aligned = lax.rem(iota((256, 256), 0), 8) == lax.rem(iota((256, 256), 1), 8)
    for j in range(3):
        for part, piece in enumerate(halves(span_in[pz, j])):
            wide = mm(spread, piece).astype(BF16)
            full = lax.dot_general(
                wide, spread, (((1,), (1,)), ((), ())), preferred_element_type=F32
            )
            full = jnp.where(aligned, full, 0.0).astype(BF16)
            if part == 0:
                span_w[:, 256 * j : 256 * j + 256] = full
                span_w[:, 768 + 256 * j : 768 + 256 * j + 256] = full
            else:
                span_w[:, 1536 + 256 * j : 1536 + 256 * j + 256] = full

    for offset in range(1, 8):
        stage_one(offset).wait_recv()
    for offset in range(1, 16):
        stage_two(offset).start()
    for p in range(16):

        @pl.when(pz == p)
        def _(p=p):
            received[p] = staged[p]

    send_forward(1, 3)
    send_beside(1, 2)
    send_beside(1, 3)
    loads[1].wait()
    for offset in range(1, 16):
        stage_two(offset).wait_recv()

    arrived = jnp.concatenate(thirds(received[...].reshape(128, 128)), axis=1)
    below = jnp.where(lane < row, 1.0, 0.0).astype(BF16)
    before = jnp.zeros((1, 128), F32)
    sources = source_block[pl.ds(me, 1), :]
    sources = ((sources & 15) * 8 + (sources >> 4)).astype(F32)
    for g in range(8):
        named = jnp.broadcast_to(sources[:, 128 * g : 128 * g + 128], (128, 128)).T
        flags = jnp.where(named == lane.astype(F32), 1.0, 0.0)
        ahead = mm(below, flags.astype(BF16)) + before
        before = before + jnp.sum(flags, axis=0, keepdims=True)
        rank = jnp.sum(flags * ahead, axis=1, keepdims=True)
        values = mm(flags.astype(BF16), arrived)
        values = values[:, :128] + values[:, 128:256] + values[:, 256:384]
        values = jnp.where((lane // 8).astype(F32) == rank, values, 0.0)
        for shift in (64, 32, 16, 8):
            values = values + pltpu.roll(values, shift, 1)
        for f in range(5):
            column = jnp.broadcast_to(values[:, f : f + 1] * gain[f], (128, 128))
            old = cur[0, f, g].reshape(128, 128)
            cur[0, f, g] = jnp.where(lane == 0, column, old).reshape(4, 32, 128)

    for q in range(4):
        send_forward(0, q)
        send_beside(0, q)

    loads[2].wait()
    loads[3].wait()

    def stream(p, carry):
        for q in range(4):
            for h in range(2):
                pieces = flux(0, *[cur[h, f, p, q] for f in range(5)])
                for f in range(5):
                    high, low = halves(pieces[f])
                    rows = pl.ds(128 * f + 32 * q, 32)
                    stream_work[rows, 128 * h : 128 * h + 128] = high
                    stream_work[rows, 256 + 128 * h : 384 + 128 * h] = low
        nt = (((1,), (1,)), ((), ()))
        term = lax.dot_general(
            stream_work[...], stream_w[:, 0:512], nt, preferred_element_type=F32
        ) + lax.dot_general(
            stream_work[:, 0:256], stream_w[:, 512:768], nt, preferred_element_type=F32
        )
        for f in range(5):
            for h in range(2):
                part = term[128 * f : 128 * f + 128, 128 * h : 128 * h + 128]
                base[h, f, p] = SECTION_DECAY * base[h, f, p] - TIME_STEP * part.reshape(
                    4, 32, 128
                )
        return carry

    lax.fori_loop(0, 8, stream, 0)

    def wall(h, q):
        own(h, q).wait()
        for offset in range(1, 8):
            forward(h, q, offset).wait_recv()

        def fill(s, carry):
            pieces = flux(1, *[got[h, q, f, s] for f in range(5)])
            for f in range(5):
                high, low = halves(pieces[f])
                work[pl.ds(32 * s, 32), 128 * f : 128 * f + 128] = high
                work[pl.ds(256 + 32 * s, 32), 128 * f : 128 * f + 128] = low
            return carry

        lax.fori_loop(0, 8, fill, 0)
        term = mm(wall_w[:, 0:512], work[pl.ds(0, 512), :]) + mm(
            wall_w[:, 512:768], work[pl.ds(0, 256), :]
        )
        for f in range(5):
            wall_out[h, q, f] = term[:, 128 * f : 128 * f + 128].reshape(8, 32, 128)
        for offset in ORDER:
            giveback(h, q, offset).start()
        for f in range(5):
            back[h, f, py, q] = wall_out[h, q, f, py]

    def span(h):
        for side in range(2):
            for i in range(4):
                beside(h, side, i).wait_recv()

        def tile(t, carry):
            rows = pl.ds(pl.multiple_of(8 * t, 8), 8)

            def fill(p, inner):
                for j in range(3):
                    if j == 1:
                        fields = [cur[h, f, p, :, rows, :] for f in range(5)]
                    else:
                        fields = [halo[j // 2, h, f, p, :, rows, :] for f in range(5)]
                    pieces = flux(2, *[field.reshape(32, 128) for field in fields])
                    for f in range(5):
                        high, low = halves(pieces[f])
                        work[pl.ds(256 * j + 32 * p, 32), 128 * f : 128 * f + 128] = high
                        work[pl.ds(768 + 256 * j + 32 * p, 32), 128 * f : 128 * f + 128] = low
                return inner

            lax.fori_loop(0, 8, fill, 0)
            term = mm(span_w[:, 0:1536], work[...]) + mm(
                span_w[:, 1536:2304], work[pl.ds(0, 768), :]
            )
            for f in range(5):
                part = term[:, 128 * f : 128 * f + 128].reshape(8, 4, 8, 128)
                base[h, f, :, :, rows, :] = base[h, f, :, :, rows, :] - TIME_STEP * part
            return carry

        lax.fori_loop(0, 4, tile, 0)

    def outputs(h, q):
        return (
            pltpu.make_async_copy(
                base.at[h, :, :, q], out_reg.at[:, :, q, :, half(h)], out_sem.at[0, h, q]
            ),
            pltpu.make_async_copy(
                got.at[h, q], out_con.at[:, :, q, :, half(h)], out_sem.at[1, h, q]
            ),
        )

    def finish(h, q):
        for offset in range(1, 8):
            giveback(h, q, offset).wait_recv()

        def join(p, carry):
            for f in range(5):
                fresh = base[h, f, p, q] - TIME_STEP * back[h, f, p, q]
                base[h, f, p, q] = fresh
                got[h, q, f, p] = cur[h, f, p, q] + SECTION_GAIN * fresh
            return carry

        lax.fori_loop(0, 8, join, 0)
        for copy in outputs(h, q):
            copy.start()

    for q in range(4):
        wall(1, q)
    span(1)
    for q in range(4):
        wall(0, q)
    span(0)
    for h in (1, 0):
        for q in range(4):
            finish(h, q)

    for offset in range(1, 8):
        stage_one(offset).wait_send()
    for offset in range(1, 16):
        stage_two(offset).wait_send()
    for h in (1, 0):
        for q in range(4):
            for offset in range(1, 8):
                forward(h, q, offset).wait_send()
                giveback(h, q, offset).wait_send()
            for side in range(2):
                beside(h, side, q).wait_send()
            for copy in outputs(h, q):
                copy.wait()


def local(
    conserved,
    register,
    stream_blocks,
    wall_matrix,
    span_blocks,
    inflow_gain,
    source_block,
    source_column,
):
    shape = (5, 8, 4, 32, 256)
    anywhere = pl.BlockSpec(memory_space=pl.ANY)
    vmem = pl.BlockSpec(memory_space=pltpu.VMEM)
    dma = pltpu.SemaphoreType.DMA
    halved = (2, 5, 8, 4, 32, 128)
    new_conserved, new_register = pl.pallas_call(
        kernel,
        out_shape=[jax.ShapeDtypeStruct(shape, F32)] * 2,
        in_specs=[
            anywhere,
            anywhere,
            vmem,
            vmem,
            vmem,
            pl.BlockSpec(memory_space=pltpu.SMEM),
            vmem,
            vmem,
        ],
        out_specs=[anywhere, anywhere],
        scratch_shapes=[
            pltpu.VMEM(halved, F32),
            pltpu.VMEM((2, 4, 5, 8, 32, 128), F32),
            pltpu.VMEM((2, 4, 5, 8, 32, 128), F32),
            pltpu.VMEM(halved, F32),
            pltpu.VMEM(halved, F32),
            pltpu.VMEM((2,) + halved, F32),
            pltpu.VMEM((1536, 640), BF16),
            pltpu.VMEM((640, 512), BF16),
            pltpu.VMEM((256, 768), BF16),
            pltpu.VMEM((256, 768), BF16),
            pltpu.VMEM((256, 2304), BF16),
            pltpu.VMEM((128, 1024), F32),
            pltpu.VMEM((8, 16, 128), F32),
            pltpu.VMEM((16, 8, 128), F32),
            pltpu.VMEM((16, 8, 128), F32),
            dma((4,)),
            dma((2, 4, 8)),
            dma((2, 4, 8)),
            dma((2, 4, 8)),
            dma((2, 4, 8)),
            dma((2, 2, 4)),
            dma((2, 2, 4)),
            dma((8,)),
            dma((8,)),
            dma((16,)),
            dma((16,)),
            dma((2, 2, 4)),
        ],
        compiler_params=pltpu.CompilerParams(
            collective_id=0, has_side_effects=True, vmem_limit_bytes=60 * 2**20
        ),
        name="section",
    )(
        conserved.reshape(shape),
        register.reshape(shape),
        stream_blocks,
        wall_matrix,
        span_blocks,
        inflow_gain,
        source_block.reshape(128, 1024),
        source_column,
    )
    return new_conserved.reshape(conserved.shape), new_register.reshape(register.shape)


def solution(mesh):
    split = P(None, "pz", "py", None)
    return jax.shard_map(
        local,
        mesh=mesh,
        in_specs=(split, split, P(), P(), P(), P(), P(), P()),
        out_specs=(split, split),
        check_vma=False,
    )
```

time: 773 us -> 199 us (0.26); the launches traced: 758 us -> 198 us
  waiting for transfers between devices: 500 us -> 0 us
  Pallas kernels: 0 us -> 188 us
  local copies, waits for them, and re-layouts: 149 us -> 10.1 us
  matrix products: 34.7 us -> 0 us
  other arithmetic: 30.7 us -> 0 us
  starting transfers between devices: 28.9 us -> 0 us
  between operations: 15 us -> 0.65 us
    all_gather x1 -> x0, waiting for transfers between devices: 368 us -> none  [local(): whole_plane = lax.all_gather(recycle, ('py', 'pz'), axis=1, tiled=True)]
    pallas_call x0 -> x1, Pallas kernels: none -> 188 us  [local(): pl.pallas_call(kernel, out_shape=[jax.ShapeDtypeStruct(shape, F32)] * 2,...]
    all_to_all x4 -> x0, waiting for transfers between devices: 132 us -> none  [the longest x1 52.1 us: local(): lax.all_to_all(current, 'py', split_axis=1, concat_axis=2, tiled=True)]
    dot_general x7 -> x0, matrix products: 34.7 us -> none  [the longest x3 17.9 us: span_derivative(): jnp.einsum('kab,fkb...->fka...', blocks[:, offset], rolled, precision=hig...]
    slice x22 -> x0, local copies, waits for them, and re-layouts: 32.7 us -> none  [the longest x2 7.59 us: local(): conserved[:, :, :, recycle_index].reshape(field_count, column_count)]
    all_to_all x7 -> x0, local copies, waits for them, and re-layouts: 29.3 us -> none  [the longest x3 17 us: local(): lax.all_to_all(span_term, 'pz', split_axis=1, concat_axis=2, tiled=True)]
    all_to_all x4 -> x0, starting transfers between devices: 28.9 us -> none  [the longest x1 10.9 us: local(): lax.all_to_all(span_term, 'pz', split_axis=1, concat_axis=2, tiled=True)]
    scatter x3 -> x0, local copies, waits for them, and re-layouts: 20.9 us -> none  [local(): current = conserved.at[:, :, :, 0].set(inlet_plane)]
  transfers between devices with their start and end apart: 5 -> 0, of which waited for: 5 -> 0; matrix products, arithmetic and copies ran while one was open for 18% -> 0% of each run, Pallas kernels for 0% -> 0%
where the time goes in v1:
time: 199 us; the launch traced here: 198 us
  Pallas kernels  188 us (94%)
  local copies, waits for them, and re-layouts  10.1 us (5%)
    pallas_call x1, Pallas kernels, local(): pl.pallas_call(kernel, out_shape=[jax.ShapeDtypeStruct(shape, F32)] * 2,...  188 us
    unnamed x5, local copies, waits for them, and re-layouts  10.1 us

profile of v1, /device:TPU:0, one launch (start us, length us, event | category | flops | bytes accessed | tf_op | source)
XLA Modules:
  0.0 198.5 jit_solution(1825687876148756437)
XLA Ops:
  0.6 1.9 copy.12
  2.6 187.7 %section.1 = (f32[5,8,4,32,256]{4,3,2,1,0:T(8,128)}, f32[5,8,4,32,256]{4,3,2,1,0:T(8,128)}) custom-call(f32[5,8,4,32,256]{4,3,2,1,0:T(8,128)} %bitcast.7, f32[5,8,4,32,256]{4,3,2,1,0:T(8,128)} %bitcast.8, f32[2,3,128,128]{3,2,1,0:T(8,128)} %stream_in.1, f32[256,256]{1,0:T(8,128)} %wall_in.1, f32[16,3,32,32]{3,2,1,0:T(8,128)} %span_in.1, f32[5]{0:T(128)} %gain.1, ...), custom_call_target="tpu_custom_call" | custom-call | tf_op jit(solution)/shard_map/section/pallas_call | solution.py:459
  190.2 0.0 copy-start
  190.2 5.8 %copy.15 = f32[5,32,32,256]{3,2,1,0:T(8,128)} copy(f32[5,32,32,256]{3,2,1,0:T(8,128)} %bitcast.10) | data formatting | bytes 10485760
  196.1 0.0 copy-done
  196.1 2.4 %copy.16 = f32[5,32,32,256]{3,2,1,0:T(8,128)} copy(f32[5,32,32,256]{3,2,1,0:T(8,128)S(1)} %bitcast.9) | data formatting | bytes 10485760
Async XLA Ops:
  190.2 5.9 %copy-start = (f32[5,8,4,32,256]{4,3,2,1,0:T(8,128)S(1)}, f32[5,8,4,32,256]{4,3,2,1,0:T(8,128)}, u32[]{:S(2)}) copy-start(f32[5,8,4,32,256]{4,3,2,1,0:T(8,128)} %get-tuple-element.5) | copy-start | bytes 15728644

commit v2 on v1

--- a/solution.py
+++ b/solution.py
@@ -14,6 +14,7 @@
 SECTION_GAIN = 15.0 / 16.0
 TIME_STEP = 0.1
 ORDER = (4, 1, 3, 5, 7, 6, 2)
+RELAYED = 2
 
 
 def flux(direction, density, first, second, third, energy):
@@ -71,6 +72,7 @@
     back,
     base,
     halo,
+    hop,
     work,
     stream_work,
     wall_w,
@@ -87,6 +89,8 @@
     br,
     hs,
     hr,
+    ps,
+    pr,
     s1s,
     s1r,
     s2s,
@@ -141,6 +145,33 @@
             src, halo.at[side, h, :, rows], hs.at[h, side, i], hr.at[h, side, i], (py, target)
         )
 
+    def passing(h, side, i):
+        rows = pl.ds(2 * i, 2)
+        src = con.at[:, rows, :, :, half(1)] if h == 1 else cur.at[0, :, rows]
+        target = lax.rem(pz + (14 if side == 0 else 2), 16)
+        return remote(src, hop.at[h, i], hs.at[h, side, i], pr.at[h, i], (py, target))
+
+    def onward(h, side, i):
+        target = lax.rem(pz + (3 if side == 0 else 13), 16)
+        return remote(
+            hop.at[h, i],
+            halo.at[side, h, :, pl.ds(2 * i, 2)],
+            ps.at[h, i],
+            hr.at[h, side, i],
+            (py, target),
+        )
+
+    wraps = [lax.rem(pz, 8) == 7, lax.rem(pz, 8) == 0]
+    relays = [lax.rem(pz, 8) == 5, lax.rem(pz, 8) == 2]
+
+    def send_onward(h, i):
+        for side in range(2):
+
+            @pl.when(relays[side])
+            def _(side=side):
+                passing(h, side, i).wait_recv()
+                onward(h, side, i).start()
+
     def send_forward(h, q):
         own(h, q).start()
         for offset in ORDER:
@@ -148,7 +179,18 @@
 
     def send_beside(h, i):
         for side in range(2):
-            beside(h, side, i).start()
+            if i < RELAYED:
+
+                @pl.when(wraps[side])
+                def _(side=side):
+                    passing(h, side, i).start()
+
+                @pl.when(jnp.logical_not(wraps[side]))
+                def _(side=side):
+                    beside(h, side, i).start()
+
+            else:
+                beside(h, side, i).start()
 
     def stage_one(offset):
         p = peer(offset)
@@ -181,8 +223,9 @@
         )
     pl.semaphore_wait(barrier, 22)
 
+    send_beside(1, 0)
     send_forward(1, 0)
-    send_beside(1, 0)
+    send_beside(1, 1)
     send_forward(1, 1)
 
     lane = iota((128, 128), 1)
@@ -236,8 +279,9 @@
         def _(p=p):
             staged[:, p, :] = picked[p]
 
+    send_onward(1, 0)
     send_forward(1, 2)
-    send_beside(1, 1)
+    send_beside(1, 2)
 
     high, low = halves(wall_in[...])
     wall_w[:, 0:256] = high
@@ -275,8 +319,8 @@
         def _(p=p):
             received[p] = staged[p]
 
+    send_onward(1, 1)
     send_forward(1, 3)
-    send_beside(1, 2)
     send_beside(1, 3)
     loads[1].wait()
     for offset in range(1, 16):
@@ -304,8 +348,8 @@
             cur[0, f, g] = jnp.where(lane == 0, column, old).reshape(4, 32, 128)
 
     for q in range(4):
+        send_beside(0, q)
         send_forward(0, q)
-        send_beside(0, q)
 
     loads[2].wait()
     loads[3].wait()
@@ -334,6 +378,8 @@
         return carry
 
     lax.fori_loop(0, 8, stream, 0)
+    for i in range(RELAYED):
+        send_onward(0, i)
 
     def wall(h, q):
         own(h, q).wait()
@@ -437,6 +483,12 @@
                 giveback(h, q, offset).wait_send()
             for side in range(2):
                 beside(h, side, q).wait_send()
+                if q < RELAYED:
+
+                    @pl.when(relays[side])
+                    def _(h=h, q=q, side=side):
+                        onward(h, side, q).wait_send()
+
             for copy in outputs(h, q):
                 copy.wait()
 
@@ -477,6 +529,7 @@
             pltpu.VMEM(halved, F32),
             pltpu.VMEM(halved, F32),
             pltpu.VMEM((2,) + halved, F32),
+            pltpu.VMEM((2, RELAYED, 5, 2, 4, 32, 128), F32),
             pltpu.VMEM((1536, 640), BF16),
             pltpu.VMEM((640, 512), BF16),
             pltpu.VMEM((256, 768), BF16),
@@ -493,6 +546,8 @@
             dma((2, 4, 8)),
             dma((2, 2, 4)),
             dma((2, 2, 4)),
+            dma((2, RELAYED)),
+            dma((2, RELAYED)),
             dma((8,)),
             dma((8,)),
             dma((16,)),

time: 199 us -> 173 us (0.87)
  Pallas kernels: 188 us -> 162 us
    pallas_call x1, Pallas kernels: 188 us -> 162 us  [local(): pl.pallas_call(kernel, out_shape=[jax.ShapeDtypeStruct(shape, F32)] * 2,...]
where the time goes in v2:
time: 173 us
  Pallas kernels  162 us (94%)
  local copies, waits for them, and re-layouts  10.1 us (6%)
    pallas_call x1, Pallas kernels, local(): pl.pallas_call(kernel, out_shape=[jax.ShapeDtypeStruct(shape, F32)] * 2,...  162 us
    unnamed x5, local copies, waits for them, and re-layouts  10.1 us

profile of v2, /device:TPU:0, one launch (start us, length us, event | category | flops | bytes accessed | tf_op | source)
XLA Modules:
  0.0 172.7 jit_solution(3386404983159395868)
XLA Ops:
  0.6 1.9 %copy.12 = s32[128,1024,1]{1,0,2:T(8,128)} copy(s32[128,1024,1]{1,2,0:T(1,128)} %param.14) | data formatting | bytes 1048576
  2.6 161.9 %section.1 = (f32[5,8,4,32,256]{4,3,2,1,0:T(8,128)}, f32[5,8,4,32,256]{4,3,2,1,0:T(8,128)}) custom-call(f32[5,8,4,32,256]{4,3,2,1,0:T(8,128)} %bitcast.7, f32[5,8,4,32,256]{4,3,2,1,0:T(8,128)} %bitcast.8, f32[2,3,128,128]{3,2,1,0:T(8,128)} %stream_in.1, f32[256,256]{1,0:T(8,128)} %wall_in.1, f32[16,3,32,32]{3,2,1,0:T(8,128)} %span_in.1, f32[5]{0:T(128)} %gain.1, ...), custom_call_target="tpu_custom_call" | custom-call | tf_op jit(solution)/shard_map/section/pallas_call | solution.py:511
  164.5 0.0 copy-start
  164.5 5.8 %copy.15 = f32[5,32,32,256]{3,2,1,0:T(8,128)} copy(f32[5,32,32,256]{3,2,1,0:T(8,128)} %bitcast.10) | data formatting | bytes 10485760
  170.4 0.0 copy-done
  170.4 2.4 %copy.16 = f32[5,32,32,256]{3,2,1,0:T(8,128)} copy(f32[5,32,32,256]{3,2,1,0:T(8,128)S(1)} %bitcast.9) | data formatting | bytes 10485760
Async XLA Ops:
  164.5 5.9 %copy-start = (f32[5,8,4,32,256]{4,3,2,1,0:T(8,128)S(1)}, f32[5,8,4,32,256]{4,3,2,1,0:T(8,128)}, u32[]{:S(2)}) copy-start(f32[5,8,4,32,256]{4,3,2,1,0:T(8,128)} %get-tuple-element.5) | copy-start | bytes 15728644

commit v3 on v2

--- a/solution.py
+++ b/solution.py
@@ -15,6 +15,7 @@
 TIME_STEP = 0.1
 ORDER = (4, 1, 3, 5, 7, 6, 2)
 RELAYED = 2
+VMEM_MIB = 50
 
 
 def flux(direction, density, first, second, third, energy):
@@ -70,7 +71,6 @@
     got,
     wall_out,
     back,
-    base,
     halo,
     hop,
     work,
@@ -95,7 +95,6 @@
     s1r,
     s2s,
     s2r,
-    out_sem,
 ):
     py, pz = lax.axis_index("py"), lax.axis_index("pz")
     me = py * 16 + pz
@@ -207,10 +206,7 @@
     loads = [
         pltpu.make_async_copy(con.at[:, :, :, :, half(h)], cur.at[h], load_sem.at[h])
         for h in (1, 0)
-    ] + [
-        pltpu.make_async_copy(reg.at[:, :, :, :, half(h)], base.at[h], load_sem.at[2 + h])
-        for h in range(2)
-    ]
+    ] + [pltpu.make_async_copy(reg, out_reg, load_sem.at[2])]
     for load in loads:
         load.start()
 
@@ -234,7 +230,7 @@
     counts = jnp.concatenate([strict, jnp.ones((128, 128), BF16)], axis=1)
     passed = jnp.zeros((128, 128), F32)
     for g in range(8):
-        mine = source_block[:, 128 * g : 128 * g + 128] == me
+        mine = source_block[:, 0, 128 * g : 128 * g + 128] == me
         ranked = mm(jnp.where(mine, 1.0, 0.0).astype(BF16), counts)
         slot_key[:, 128 * g : 128 * g + 128] = jnp.where(mine, ranked[:, :128] + passed, -1.0)
         passed = passed + ranked[:, 128:]
@@ -329,7 +325,7 @@
     arrived = jnp.concatenate(thirds(received[...].reshape(128, 128)), axis=1)
     below = jnp.where(lane < row, 1.0, 0.0).astype(BF16)
     before = jnp.zeros((1, 128), F32)
-    sources = source_block[pl.ds(me, 1), :]
+    sources = source_block[me]
     sources = ((sources & 15) * 8 + (sources >> 4)).astype(F32)
     for g in range(8):
         named = jnp.broadcast_to(sources[:, 128 * g : 128 * g + 128], (128, 128)).T
@@ -352,7 +348,6 @@
         send_forward(0, q)
 
     loads[2].wait()
-    loads[3].wait()
 
     def stream(p, carry):
         for q in range(4):
@@ -372,8 +367,9 @@
         for f in range(5):
             for h in range(2):
                 part = term[128 * f : 128 * f + 128, 128 * h : 128 * h + 128]
-                base[h, f, p] = SECTION_DECAY * base[h, f, p] - TIME_STEP * part.reshape(
-                    4, 32, 128
+                old = out_reg[f, p, :, :, half(h)]
+                out_reg[f, p, :, :, half(h)] = (
+                    SECTION_DECAY * old - TIME_STEP * part.reshape(4, 32, 128)
                 )
         return carry
 
@@ -432,20 +428,11 @@
             )
             for f in range(5):
                 part = term[:, 128 * f : 128 * f + 128].reshape(8, 4, 8, 128)
-                base[h, f, :, :, rows, :] = base[h, f, :, :, rows, :] - TIME_STEP * part
+                old = out_reg[f, :, :, rows, half(h)]
+                out_reg[f, :, :, rows, half(h)] = old - TIME_STEP * part
             return carry
 
         lax.fori_loop(0, 4, tile, 0)
-
-    def outputs(h, q):
-        return (
-            pltpu.make_async_copy(
-                base.at[h, :, :, q], out_reg.at[:, :, q, :, half(h)], out_sem.at[0, h, q]
-            ),
-            pltpu.make_async_copy(
-                got.at[h, q], out_con.at[:, :, q, :, half(h)], out_sem.at[1, h, q]
-            ),
-        )
 
     def finish(h, q):
         for offset in range(1, 8):
@@ -453,14 +440,12 @@
 
         def join(p, carry):
             for f in range(5):
-                fresh = base[h, f, p, q] - TIME_STEP * back[h, f, p, q]
-                base[h, f, p, q] = fresh
-                got[h, q, f, p] = cur[h, f, p, q] + SECTION_GAIN * fresh
+                fresh = out_reg[f, p, q, :, half(h)] - TIME_STEP * back[h, f, p, q]
+                out_reg[f, p, q, :, half(h)] = fresh
+                out_con[f, p, q, :, half(h)] = cur[h, f, p, q] + SECTION_GAIN * fresh
             return carry
 
         lax.fori_loop(0, 8, join, 0)
-        for copy in outputs(h, q):
-            copy.start()
 
     for q in range(4):
         wall(1, q)
@@ -488,9 +473,6 @@
                     @pl.when(relays[side])
                     def _(h=h, q=q, side=side):
                         onward(h, side, q).wait_send()
-
-            for copy in outputs(h, q):
-                copy.wait()
 
 
 def local(
@@ -510,7 +492,7 @@
     halved = (2, 5, 8, 4, 32, 128)
     new_conserved, new_register = pl.pallas_call(
         kernel,
-        out_shape=[jax.ShapeDtypeStruct(shape, F32)] * 2,
+        out_shape=[pltpu.VMEM(shape, F32)] * 2,
         in_specs=[
             anywhere,
             anywhere,
@@ -521,12 +503,11 @@
             vmem,
             vmem,
         ],
-        out_specs=[anywhere, anywhere],
+        out_specs=[vmem, vmem],
         scratch_shapes=[
             pltpu.VMEM(halved, F32),
             pltpu.VMEM((2, 4, 5, 8, 32, 128), F32),
             pltpu.VMEM((2, 4, 5, 8, 32, 128), F32),
-            pltpu.VMEM(halved, F32),
             pltpu.VMEM(halved, F32),
             pltpu.VMEM((2,) + halved, F32),
             pltpu.VMEM((2, RELAYED, 5, 2, 4, 32, 128), F32),
@@ -552,10 +533,9 @@
             dma((8,)),
             dma((16,)),
             dma((16,)),
-            dma((2, 2, 4)),
         ],
         compiler_params=pltpu.CompilerParams(
-            collective_id=0, has_side_effects=True, vmem_limit_bytes=60 * 2**20
+            collective_id=0, has_side_effects=True, vmem_limit_bytes=VMEM_MIB * 2**20
         ),
         name="section",
     )(
@@ -565,7 +545,7 @@
         wall_matrix,
         span_blocks,
         inflow_gain,
-        source_block.reshape(128, 1024),
+        jnp.swapaxes(source_block, 1, 2),
         source_column,
     )
     return new_conserved.reshape(conserved.shape), new_register.reshape(register.shape)

time: 173 us -> 166 us (0.960)
  local copies, waits for them, and re-layouts: 10.1 us -> 4.72 us
    unnamed x5 -> x2, local copies, waits for them, and re-layouts: 10.1 us -> 4.72 us
where the time goes in v3:
time: 166 us
  Pallas kernels  161 us (97%)
  local copies, waits for them, and re-layouts  4.72 us (3%)
    pallas_call x1, Pallas kernels, local(): pl.pallas_call(kernel, out_shape=[pltpu.VMEM(shape, F32)] * 2, in_specs=[...  161 us
    unnamed x2, local copies, waits for them, and re-layouts  4.72 us

profile of v3, /device:TPU:0, one launch (start us, length us, event | category | flops | bytes accessed | tf_op | source)
XLA Modules:
  0.0 166.3 jit_solution(9218003336893305688)
XLA Ops:
  0.6 161.0 %section.1 = (f32[5,8,4,32,256]{4,3,2,1,0:T(8,128)S(1)}, f32[5,8,4,32,256]{4,3,2,1,0:T(8,128)S(1)}) custom-call(f32[5,8,4,32,256]{4,3,2,1,0:T(8,128)} %bitcast.7, f32[5,8,4,32,256]{4,3,2,1,0:T(8,128)} %bitcast.8, f32[2,3,128,128]{3,2,1,0:T(8,128)} %stream_in.1, f32[256,256]{1,0:T(8,128)} %wall_in.1, f32[16,3,32,32]{3,2,1,0:T(8,128)} %span_in.1, f32[5]{0:T(128)} %gain.1, ...), custom_call_target="tpu_custom_call" | custom-call | tf_op jit(solution)/shard_map/section/pallas_call | solution.py:493
  161.6 2.4 %copy.12 = f32[5,32,32,256]{3,2,1,0:T(8,128)} copy(f32[5,32,32,256]{3,2,1,0:T(8,128)S(1)} %bitcast.6) | data formatting | bytes 10485760
  164.0 2.4 %copy.13 = f32[5,32,32,256]{3,2,1,0:T(8,128)} copy(f32[5,32,32,256]{3,2,1,0:T(8,128)S(1)} %bitcast.5) | data formatting | bytes 10485760

commit v4 on v3

--- a/solution.py
+++ b/solution.py
@@ -13,7 +13,7 @@
 SECTION_DECAY = -5.0 / 9.0
 SECTION_GAIN = 15.0 / 16.0
 TIME_STEP = 0.1
-ORDER = (4, 1, 3, 5, 7, 6, 2)
+ORDER = (6, 2, 5, 7, 1, 3, 4)
 RELAYED = 2
 VMEM_MIB = 50
 
@@ -449,9 +449,9 @@
 
     for q in range(4):
         wall(1, q)
-    span(1)
     for q in range(4):
         wall(0, q)
+    span(1)
     span(0)
     for h in (1, 0):
         for q in range(4):

time: 166 us -> 165 us (level)
  Pallas kernels: 161 us -> 159 us
where the time goes in v4:
time: 165 us
  Pallas kernels  159 us (96%)
  local copies, waits for them, and re-layouts  4.72 us (3%)
    pallas_call x1, Pallas kernels, local(): pl.pallas_call(kernel, out_shape=[pltpu.VMEM(shape, F32)] * 2, in_specs=[...  159 us
    unnamed x2, local copies, waits for them, and re-layouts  4.72 us

profile of v4, /device:TPU:0, one launch (start us, length us, event | category | flops | bytes accessed | tf_op | source)
XLA Modules:
  0.0 164.8 jit_solution(2310572790401713508)
XLA Ops:
  0.6 159.4 %section.1 = (f32[5,8,4,32,256]{4,3,2,1,0:T(8,128)S(1)}, f32[5,8,4,32,256]{4,3,2,1,0:T(8,128)S(1)}) custom-call(f32[5,8,4,32,256]{4,3,2,1,0:T(8,128)} %bitcast.7, f32[5,8,4,32,256]{4,3,2,1,0:T(8,128)} %bitcast.8, f32[2,3,128,128]{3,2,1,0:T(8,128)} %stream_in.1, f32[256,256]{1,0:T(8,128)} %wall_in.1, f32[16,3,32,32]{3,2,1,0:T(8,128)} %span_in.1, f32[5]{0:T(128)} %gain.1, ...), custom_call_target="tpu_custom_call" | custom-call | tf_op jit(solution)/shard_map/section/pallas_call | solution.py:493
  160.0 2.4 %copy.12 = f32[5,32,32,256]{3,2,1,0:T(8,128)} copy(f32[5,32,32,256]{3,2,1,0:T(8,128)S(1)} %bitcast.6) | data formatting | bytes 10485760
  162.4 2.4 %copy.13 = f32[5,32,32,256]{3,2,1,0:T(8,128)} copy(f32[5,32,32,256]{3,2,1,0:T(8,128)S(1)} %bitcast.5) | data formatting | bytes 10485760

commit v5 on v4

--- a/solution.py
+++ b/solution.py
@@ -473,6 +473,18 @@
                     @pl.when(relays[side])
                     def _(h=h, q=q, side=side):
                         onward(h, side, q).wait_send()
+
+
+def store(con, reg, out_con, out_reg, sems):
+    copies = [
+        pltpu.make_async_copy(src.at[f], dst.at[f], sems.at[n, f])
+        for f in range(5)
+        for n, (src, dst) in enumerate(((con, out_con), (reg, out_reg)))
+    ]
+    for copy in copies:
+        copy.start()
+    for copy in copies:
+        copy.wait()
 
 
 def local(
@@ -548,6 +560,15 @@
         jnp.swapaxes(source_block, 1, 2),
         source_column,
     )
+    new_conserved, new_register = pl.pallas_call(
+        store,
+        out_shape=[jax.ShapeDtypeStruct(shape, F32)] * 2,
+        in_specs=[anywhere, anywhere],
+        out_specs=[anywhere, anywhere],
+        scratch_shapes=[dma((2, 5))],
+        compiler_params=pltpu.CompilerParams(vmem_limit_bytes=2**20),
+        name="store",
+    )(new_conserved, new_register)
     return new_conserved.reshape(conserved.shape), new_register.reshape(register.shape)
 
 

time: 165 us -> 164 us (level)
  local copies, waits for them, and re-layouts: 4.72 us -> 0 us
  Pallas kernels: 159 us -> 163 us
    unnamed x2 -> x0, local copies, waits for them, and re-layouts: 4.72 us -> none
    pallas_call x0 -> x1, Pallas kernels: none -> 4.02 us  [local(): pl.pallas_call(store, out_shape=[jax.ShapeDtypeStruct(shape, F32)] * 2, i...]
where the time goes in v5:
time: 164 us
  Pallas kernels  163 us (99%)
    pallas_call x1, Pallas kernels, local(): pl.pallas_call(kernel, out_shape=[pltpu.VMEM(shape, F32)] * 2, in_specs=[...  159 us
    pallas_call x1, Pallas kernels, local(): pl.pallas_call(store, out_shape=[jax.ShapeDtypeStruct(shape, F32)] * 2, i...  4.02 us

profile of v5, /device:TPU:0, one launch (start us, length us, event | category | flops | bytes accessed | tf_op | source)
XLA Modules:
  0.0 164.2 jit_solution(15010229395680093799)
XLA Ops:
  0.6 159.4 %section.1 = (f32[5,8,4,32,256]{4,3,2,1,0:T(8,128)S(1)}, f32[5,8,4,32,256]{4,3,2,1,0:T(8,128)S(1)}) custom-call(f32[5,8,4,32,256]{4,3,2,1,0:T(8,128)} %bitcast.5, f32[5,8,4,32,256]{4,3,2,1,0:T(8,128)} %bitcast.6, f32[2,3,128,128]{3,2,1,0:T(8,128)} %stream_in.1, f32[256,256]{1,0:T(8,128)} %wall_in.1, f32[16,3,32,32]{3,2,1,0:T(8,128)} %span_in.1, f32[5]{0:T(128)} %gain.1, ...), custom_call_target="tpu_custom_call" | custom-call | tf_op jit(solution)/shard_map/section/pallas_call | solution.py:505
  160.0 4.0 %store.1 = (f32[5,8,4,32,256]{4,3,2,1,0:T(8,128)}, f32[5,8,4,32,256]{4,3,2,1,0:T(8,128)}) custom-call(f32[5,8,4,32,256]{4,3,2,1,0:T(8,128)S(1)} %get-tuple-element.6.con, f32[5,8,4,32,256]{4,3,2,1,0:T(8,128)S(1)} %get-tuple-element.7.reg), custom_call_target="tpu_custom_call" | custom-call | tf_op jit(solution)/shard_map/store/pallas_call | solution.py:563
